TPU v7x, 128 devices: a whole 4x4x4 slice. The times are simulated.
128 devices in a mesh: step: 8 (over y_lo, z), space: 16 (over x, y_hi, core).
Axes of the slice: x: 4, y: 4 (y_hi: 2, y_lo: 2; y = y_hi * 2 + y_lo), z: 4, core: 2. Of those that a mesh axis runs over, the one named last changes fastest.
Arguments:
- snapshots: float32 [8, 16, 256, 256], P('step', 'space'), may hold values from 0.25 to 2
- drift: bfloat16 [8, 3, 16, 256, 256], P('step', None, 'space'), may hold values from -3 to 3
- pair_table: int32 [16, 2], P('step'), may hold values from 0 to 7
- plan: int32 [16, 4], P('step'), may hold values from 0 to 7
Outputs:
- final_density: float32 [16, 16, 256, 256], P('step', 'space')
- adjoint_start: float32 [16, 16, 256, 256], P('step', 'space')
- drift_grad: float32 [8, 3, 16, 256, 256], P('step', None, 'space')
All inputs are finite; a program needn't handle non-finite values.
Results may differ from a plain program's by a relative error of at most 0.0003.
Values may be sent and summed in bfloat16 or wider, within the bound.
No kernel may reach another device: no remote copies, remote signals or barrier semaphores. Data moves between devices by JAX's collectives and lax.ppermute only.
A program may use at most 64 MiB of HBM per device.

v0:
```python
import jax
import jax.numpy as jnp
from jax import lax
from jax.sharding import PartitionSpec as P

WIN = 4


time_step = 0.1
diffusion = 1.0


def with_halo(cells, sides, width):
    for axis, dim in sides:
        count = lax.axis_size(axis)
        ends = count - 1
        head = lax.slice_in_dim(cells, 0, width, axis=dim)
        tail = lax.slice_in_dim(cells, cells.shape[dim] - width, cells.shape[dim], axis=dim)
        cells = jnp.concatenate(
            [
                lax.ppermute(tail, axis, [(i, (i + 1) % count) for i in range(ends)]),
                cells,
                lax.ppermute(head, axis, [((i + 1) % count, i) for i in range(ends)]),
            ],
            axis=dim,
        )
    return cells


def diff_plane(field, axis):
    return (jnp.roll(field, -1, axis) - jnp.roll(field, 1, axis)) * 0.5


def diff_depth(padded):
    return (padded[:, 2:] - padded[:, :-2]) * 0.5


def laplace(field, padded):
    total = padded[:, 2:] + padded[:, :-2]
    total = total + jnp.roll(field, -1, 2) + jnp.roll(field, 1, 2)
    total = total + jnp.roll(field, -1, 3) + jnp.roll(field, 1, 3)
    return total - 6.0 * field


def local(snapshots, drift, pair_table, plan):
    num_steps = drift.shape[0] * lax.axis_size("step")
    gathered_snaps = lax.all_gather(snapshots, "step", axis=0, tiled=True)
    density = gathered_snaps[pair_table[:, 0]]
    targets = gathered_snaps[pair_table[:, 1]]
    step_ids = jnp.arange(num_steps, dtype=jnp.int32)
    states = []
    velocities = []
    for index in range(WIN):
        wanted = plan[:, index]
        piece = lax.all_gather(drift, "step", axis=0, tiled=True)
        count = piece.shape[0]
        add_onehot = (wanted[:, None] == jnp.arange(count, dtype=jnp.int32)[None, :]).astype(
            jnp.float32
        )
        velocity = jnp.einsum(
            "ps,sczyx->pczyx",
            add_onehot,
            piece.astype(jnp.float32),
            precision=lax.Precision.HIGHEST,
        )
        velocities.append(velocity)
        speed = velocity
        states.append(density)
        flux = speed[:, 2] * density
        stacked = jnp.stack([density, flux])
        padded_both = with_halo(stacked, (("space", 2),), 1)
        change = (
            diffusion * laplace(density, padded_both[0])
            - diff_plane(speed[:, 0] * density, 3)
            - diff_plane(speed[:, 1] * density, 2)
            - diff_depth(padded_both[1])
        )
        density = density + time_step * change
    adjoint = density - targets
    partial_value = jnp.zeros((num_steps,) + drift.shape[1:], jnp.float32)
    for index in reversed(range(WIN)):
        speed = velocities[index]
        padded = with_halo(adjoint, (("space", 1),), 1)
        slope_x = diff_plane(adjoint, 3)
        slope_y = diff_plane(adjoint, 2)
        slope_z = diff_depth(padded)
        change = (
            diffusion * laplace(adjoint, padded)
            + speed[:, 0] * slope_x
            + speed[:, 1] * slope_y
            + speed[:, 2] * slope_z
        )
        term = time_step * states[index][:, None] * jnp.stack([slope_x, slope_y, slope_z], axis=1)
        onehot = (plan[:, index][:, None] == step_ids[None, :]).astype(jnp.float32)
        partial_value = partial_value + jnp.einsum(
            "ps,pczyx->sczyx", onehot, term, precision=lax.Precision.HIGHEST
        )
        adjoint = adjoint + time_step * change
    owned = lax.psum_scatter(partial_value, "step", scatter_dimension=0, tiled=True)
    return (density, adjoint, owned)


def solution(mesh):
    return jax.shard_map(
        local,
        mesh=mesh,
        in_specs=(
            P("step", "space", None, None),
            P("step", None, "space", None, None),
            P("step", None),
            P("step", None),
        ),
        out_specs=(
            P("step", "space", None, None),
            P("step", "space", None, None),
            P("step", None, "space", None, None),
        ),
        check_vma=False,
    )
```

profile of v0, /device:TPU:1, one launch (start us, length us, event | category | flops | bytes accessed | tf_op | source)
XLA Modules:
  0.0 407.9 jit_solution(15273287047168198019)
XLA Ops:
  10.7 38.1 %all-gather.3.cloned.1.call-done = f32[8,1,256,256]{3,2,1,0:T(8,128)} async-done(((f32[1,1,256,256]{3,2,1,0:T(8,128)}), f32[8,1,256,256]{3,2,1,0:T(8,128)}) %all-gather.3.cloned.1.call-update) | async-done | bytes 2097168 | tf_op jit(solution)/shard_map/all_gather | solution.py:47
  53.6 43.3 %all-gather.5.cloned.1.call-done = bf16[8,3,1,256,256]{4,3,2,1,0:T(8,128)(2,1)} async-done(((bf16[1,3,1,256,256]{4,3,2,1,0:T(8,128)(2,1)}), bf16[8,3,1,256,256]{4,3,2,1,0:T(8,128)(2,1)}) %all-gather.5.cloned.1.call-update) | async-done | bytes 3145744 | tf_op jit(solution)/shard_map/all_gather | solution.py:55
  97.0 4.0 fusion.6
  102.0 4.9 %collective-permute-start.1 = (f32[2,2,1,256,256]{4,1,3,2,0:T(2,128)S(1)}, f32[2,2,1,256,256]{4,1,3,2,0:T(2,128)S(1)}, u32[]{:S(2)}, u32[]{:S(2)}) collective-permute-start(f32[2,2,1,256,256]{4,1,3,2,0:T(2,128)S(1)} %pad_maximum_fusion.4), channel_id=1, source_target_pairs={{1,0},{2,1},{3,2},{4,3},{5,4},{6,5},{7,6},{8,7},{9,8},{10,9},{11,1... | collective-permute-start | bytes 3145736 | tf_op jit(solution)/shard_map/ppermute | solution.py:23
  107.0 4.8 %collective-permute-start = (f32[2,2,1,256,256]{4,1,3,2,0:T(2,128)S(1)}, f32[2,2,1,256,256]{4,1,3,2,0:T(2,128)S(1)}, u32[]{:S(2)}, u32[]{:S(2)}) collective-permute-start(f32[2,2,1,256,256]{4,1,3,2,0:T(2,128)S(1)} %pad_maximum_fusion.4), channel_id=1, source_target_pairs={{0,1},{1,2},{2,3},{3,4},{4,5},{5,6},{6,7},{7,8},{8,9},{9,10},{10,1... | collective-permute-start | bytes 3145736 | tf_op jit(solution)/shard_map/ppermute | solution.py:21
  122.0 9.0 %collective-permute-done = f32[2,2,1,256,256]{4,1,3,2,0:T(2,128)S(1)} collective-permute-done((f32[2,2,1,256,256]{4,1,3,2,0:T(2,128)S(1)}, f32[2,2,1,256,256]{4,1,3,2,0:T(2,128)S(1)}, u32[]{:S(2)}, u32[]{:S(2)}) %collective-permute-start) | collective-permute-done | bytes 1048608 | tf_op jit(solution)/shard_map/ppermute | solution.py:21
  133.9 4.0 multiply_bitcast_fusion.1
  141.3 5.9 %collective-permute-start.2 = (f32[2,2,1,256,256]{4,1,3,2,0:T(2,128)S(1)}, f32[2,2,1,256,256]{4,1,3,2,0:T(2,128)S(1)}, u32[]{:S(2)}, u32[]{:S(2)}) collective-permute-start(f32[2,2,1,256,256]{4,1,3,2,0:T(2,128)S(1)} %pad_maximum_fusion.5), channel_id=1, source_target_pairs={{0,1},{1,2},{2,3},{3,4},{4,5},{5,6},{6,7},{7,8},{8,9},{9,10},{10,1... | collective-permute-start | bytes 3145736 | tf_op jit(solution)/shard_map/ppermute | solution.py:21
  149.6 8.2 %collective-permute-done.3 = f32[2,2,1,256,256]{4,1,3,2,0:T(2,128)S(1)} collective-permute-done((f32[2,2,1,256,256]{4,1,3,2,0:T(2,128)S(1)}, f32[2,2,1,256,256]{4,1,3,2,0:T(2,128)S(1)}, u32[]{:S(2)}, u32[]{:S(2)}) %collective-permute-start.3) | collective-permute-done | bytes 1048608 | tf_op jit(solution)/shard_map/ppermute | solution.py:23
  162.7 4.1 %multiply_bitcast_fusion.2 = (f32[2,256,256]{2,0,1:T(2,128)S(1)}, f32[2,1,256,256]{3,0,2,1:T(2,128)S(1)}) fusion(f32[2,1,256,256]{3,0,2,1:T(2,128)S(1)} %get-tuple-element.23, f32[2,3,256,256]{3,0,2,1:T(2,128)S(1)} %get-tuple-element.31, f32[2,1,255,256]{3,0,2,1:T(2,128)S(1)} %get-tuple-element.135, f32[2,1,1,256]{3,0,2,1:T(2,128)S(1)} %get-tuple-element.137, ...), kind=kLoop, calls=%fused_computation.164 | loop fusion | flops 3538944 | bytes 7864320 | tf_op jit(solution)/shard_map/mul | solution.py:93
  170.2 6.1 %collective-permute-start.4 = (f32[2,2,1,256,256]{4,1,3,2,0:T(2,128)S(1)}, f32[2,2,1,256,256]{4,1,3,2,0:T(2,128)S(1)}, u32[]{:S(2)}, u32[]{:S(2)}) collective-permute-start(f32[2,2,1,256,256]{4,1,3,2,0:T(2,128)S(1)} %pad_maximum_fusion.6), channel_id=1, source_target_pairs={{0,1},{1,2},{2,3},{3,4},{4,5},{5,6},{6,7},{7,8},{8,9},{9,10},{10,1... | collective-permute-start | bytes 3145736 | tf_op jit(solution)/shard_map/ppermute | solution.py:21
  178.7 8.0 %collective-permute-done.5 = f32[2,2,1,256,256]{4,1,3,2,0:T(2,128)S(1)} collective-permute-done((f32[2,2,1,256,256]{4,1,3,2,0:T(2,128)S(1)}, f32[2,2,1,256,256]{4,1,3,2,0:T(2,128)S(1)}, u32[]{:S(2)}, u32[]{:S(2)}) %collective-permute-start.5) | collective-permute-done | bytes 1048608 | tf_op jit(solution)/shard_map/ppermute | solution.py:23
  186.7 7.9 %collective-permute-done.4 = f32[2,2,1,256,256]{4,1,3,2,0:T(2,128)S(1)} collective-permute-done((f32[2,2,1,256,256]{4,1,3,2,0:T(2,128)S(1)}, f32[2,2,1,256,256]{4,1,3,2,0:T(2,128)S(1)}, u32[]{:S(2)}, u32[]{:S(2)}) %collective-permute-start.4) | collective-permute-done | bytes 1048608 | tf_op jit(solution)/shard_map/ppermute | solution.py:21
  197.4 4.1 %multiply_bitcast_fusion.3 = (f32[2,256,256]{2,0,1:T(2,128)S(1)}, f32[2,1,256,256]{3,0,2,1:T(2,128)S(1)}) fusion(f32[2,1,256,256]{3,0,2,1:T(2,128)S(1)} %get-tuple-element.19, f32[2,3,256,256]{3,0,2,1:T(2,128)S(1)} %get-tuple-element.29, f32[2,1,255,256]{3,0,2,1:T(2,128)S(1)} %get-tuple-element.119, f32[2,1,1,256]{3,0,2,1:T(2,128)S(1)} %get-tuple-element.121, ...), kind=kLoop, calls=%fused_computation.165 | loop fusion | flops 3538944 | bytes 7864320 | tf_op jit(solution)/shard_map/mul | solution.py:93
  204.9 6.1 %collective-permute-start.6 = (f32[2,2,1,256,256]{4,1,3,2,0:T(2,128)S(1)}, f32[2,2,1,256,256]{4,1,3,2,0:T(2,128)S(1)}, u32[]{:S(2)}, u32[]{:S(2)}) collective-permute-start(f32[2,2,1,256,256]{4,1,3,2,0:T(2,128)S(1)} %pad_maximum_fusion.7), channel_id=1, source_target_pairs={{0,1},{1,2},{2,3},{3,4},{4,5},{5,6},{6,7},{7,8},{8,9},{9,10},{10,1... | collective-permute-start | bytes 3145736 | tf_op jit(solution)/shard_map/ppermute | solution.py:21
  213.4 7.9 %collective-permute-done.7 = f32[2,2,1,256,256]{4,1,3,2,0:T(2,128)S(1)} collective-permute-done((f32[2,2,1,256,256]{4,1,3,2,0:T(2,128)S(1)}, f32[2,2,1,256,256]{4,1,3,2,0:T(2,128)S(1)}, u32[]{:S(2)}, u32[]{:S(2)}) %collective-permute-start.7) | collective-permute-done | bytes 1048608 | tf_op jit(solution)/shard_map/ppermute | solution.py:23
  226.3 4.0 bitcast_subtract_fusion
  230.2 5.9 %collective-permute-start.9 = (f32[2,1,256,256]{3,0,2,1:T(2,128)S(1)}, f32[2,1,256,256]{3,0,2,1:T(2,128)S(1)}, u32[]{:S(2)}, u32[]{:S(2)}) collective-permute-start(f32[2,1,256,256]{3,0,2,1:T(2,128)S(1)} %get-tuple-element.24), channel_id=1, source_target_pairs={{0,1},{1,2},{2,3},{3,4},{4,5},{5,6},{6,7},{7,8},{8,9},{9,10},{10,1... | collective-permute-start | bytes 1572872 | tf_op jit(solution)/shard_map/ppermute | solution.py:21
  242.3 5.9 %collective-permute-done.8 = f32[2,1,256,256]{3,0,2,1:T(2,128)S(1)} collective-permute-done((f32[2,1,256,256]{3,0,2,1:T(2,128)S(1)}, f32[2,1,256,256]{3,0,2,1:T(2,128)S(1)}, u32[]{:S(2)}, u32[]{:S(2)}) %collective-permute-start.8) | collective-permute-done | bytes 524320 | tf_op jit(solution)/shard_map/ppermute | solution.py:23
  248.2 2.9 subtract_multiply_fusion.11
  257.7 4.7 %fusion.12 = f32[8,3,256,256]{3,0,2,1:T(8,128)S(1)} fusion(f32[2,1,256,256]{3,0,2,1:T(2,128)S(1)} %get-tuple-element.52, f32[2,1,256,256]{3,0,2,1:T(2,128)S(1)} %subtract_multiply_fusion.10, f32[2,1,256,256]{3,0,2,1:T(2,128)S(1)} %get-tuple-element.47, f32[2,256,256]{2,0,1:T(2,128)S(1)} %get-tuple-element.20, s32[2]{0:T(128)S(1)} %get-tuple-element.14), kind=kOutput, calls=%fused_computation.28 | convolution fusion | flops 38928400 | bytes 8388616 | tf_op jit(solution)/shard_map/ps,pczyx->sczyx/dot_general | solution.py:95
  262.4 8.0 %collective-permute-done.10 = f32[2,1,256,256]{3,0,2,1:T(2,128)S(1)} collective-permute-done((f32[2,1,256,256]{3,0,2,1:T(2,128)S(1)}, f32[2,1,256,256]{3,0,2,1:T(2,128)S(1)}, u32[]{:S(2)}, u32[]{:S(2)}) %collective-permute-start.10) | collective-permute-done | bytes 524320 | tf_op jit(solution)/shard_map/ppermute | solution.py:23
  270.4 3.0 subtract_multiply_fusion.8
  279.6 4.7 %fusion.17 = f32[8,3,256,256]{3,0,2,1:T(8,128)S(1)} fusion(f32[2,1,256,256]{3,0,2,1:T(2,128)S(1)} %get-tuple-element.53, f32[2,1,256,256]{3,0,2,1:T(2,128)S(1)} %subtract_multiply_fusion.7, f32[2,1,256,256]{3,0,2,1:T(2,128)S(1)} %get-tuple-element.45, f32[2,256,256]{2,0,1:T(2,128)S(1)} %get-tuple-element.18, s32[2]{0:T(128)S(1)} %get-tuple-element.17), kind=kOutput, calls=%fused_computation.34 | convolution fusion | flops 38928400 | bytes 8388616 | tf_op jit(solution)/shard_map/ps,pczyx->sczyx/dot_general | solution.py:95
  284.3 4.2 %collective-permute-done.12 = f32[2,1,256,256]{3,0,2,1:T(2,128)S(1)} collective-permute-done((f32[2,1,256,256]{3,0,2,1:T(2,128)S(1)}, f32[2,1,256,256]{3,0,2,1:T(2,128)S(1)}, u32[]{:S(2)}, u32[]{:S(2)}) %collective-permute-start.12) | collective-permute-done | bytes 524320 | tf_op jit(solution)/shard_map/ppermute | solution.py:23
  288.5 3.0 subtract_multiply_fusion.5
  297.8 4.7 %fusion.22 = f32[8,3,256,256]{3,0,2,1:T(8,128)S(1)} fusion(f32[2,1,256,256]{3,0,2,1:T(2,128)S(1)} %get-tuple-element.51, f32[2,1,256,256]{3,0,2,1:T(2,128)S(1)} %subtract_multiply_fusion.4, f32[2,1,256,256]{3,0,2,1:T(2,128)S(1)} %get-tuple-element.49, f32[2,256,256]{2,0,1:T(2,128)S(1)} %get-tuple-element.22, s32[2]{0:T(128)S(1)} %get-tuple-element.15), kind=kOutput, calls=%fused_computation.40 | convolution fusion | flops 38928400 | bytes 8388616 | tf_op jit(solution)/shard_map/ps,pczyx->sczyx/dot_general | solution.py:95
  302.5 4.1 %collective-permute-done.14 = f32[2,1,256,256]{3,0,2,1:T(2,128)S(1)} collective-permute-done((f32[2,1,256,256]{3,0,2,1:T(2,128)S(1)}, f32[2,1,256,256]{3,0,2,1:T(2,128)S(1)}, u32[]{:S(2)}, u32[]{:S(2)}) %collective-permute-start.14) | collective-permute-done | bytes 524320 | tf_op jit(solution)/shard_map/ppermute | solution.py:23
  306.7 3.2 subtract_multiply_fusion.2
  309.8 6.0 %add_bitcast_fusion = f32[8,3,1,256,256]{4,0,3,1,2:T(8,128)S(1)} fusion(f32[8,3,256,256]{3,0,2,1:T(8,128)S(1)} %fusion.22, f32[8,3,256,256]{3,0,2,1:T(8,128)S(1)} %fusion.12, f32[8,3,256,256]{3,0,2,1:T(8,128)S(1)} %fusion.17, f32[2,1,256,256]{3,0,2,1:T(2,128)S(1)} %get-tuple-element.54, f32[2,1,256,256]{3,0,2,1:T(2,128)S(1)} %subtract_multiply_fusion.1, ...), kind=kOutput, calls=%fused_computation.2 | convolution fusion | flops 43646992 | bytes 27262984 | tf_op jit(solution)/shard_map/ps,pczyx->sczyx/dot_general | solution.py:95
  315.8 4.6 %copy.29 = f32[8,3,1,256,256]{4,3,2,1,0:T(8,128)} copy(f32[8,3,1,256,256]{4,0,3,1,2:T(8,128)S(1)} %add_bitcast_fusion) | data formatting | bytes 12582912 | tf_op jit(solution)/shard_map/add | solution.py:95
  322.1 79.0 %reduce-scatter.2.cloned.1.call-done = f32[1,3,1,256,256]{4,3,2,1,0:T(8,128)} async-done(((f32[8,3,1,256,256]{4,3,2,1,0:T(8,128)}), f32[1,3,1,256,256]{4,3,2,1,0:T(8,128)}) %reduce-scatter.2.cloned.1.call-update) | async-done | bytes 786448 | tf_op jit(solution)/shard_map/reduce_scatter | solution.py:99
  (102 shorter events, 78.7 us)
Async XLA Ops:
  7.2 41.7 %all-gather.3.cloned.1.call-start = ((), (), s32[]{:S(2)}) async-start(), calls=%async_computation.1 | async-start | bytes 2359296 | tf_op jit(solution)/shard_map/all_gather | solution.py:47
  7.9 89.1 %all-gather.5.cloned.1.call-start = ((), (), s32[]{:S(2)}) async-start(), calls=%async_computation.2 | async-start | bytes 3538944 | tf_op jit(solution)/shard_map/all_gather | solution.py:55
  8.6 392.4 %reduce-scatter.2.cloned.1.call-start = ((), (), s32[]{:S(2)}) async-start(), calls=%async_computation.3 | async-start | bytes 7077888 | tf_op jit(solution)/shard_map/reduce_scatter | solution.py:99
  102.0 20.0 %collective-permute-start.1 = (f32[2,2,1,256,256]{4,1,3,2,0:T(2,128)S(1)}, f32[2,2,1,256,256]{4,1,3,2,0:T(2,128)S(1)}, u32[]{:S(2)}, u32[]{:S(2)}) collective-permute-start(f32[2,2,1,256,256]{4,1,3,2,0:T(2,128)S(1)} %pad_maximum_fusion.4), channel_id=1, source_target_pairs={{1,0},{2,1},{3,2},{4,3},{5,4},{6,5},{7,6},{8,7},{9,8},{10,9},{11,1... | collective-permute-start | bytes 3145736 | tf_op jit(solution)/shard_map/ppermute | solution.py:23
  107.0 24.1 %collective-permute-start = (f32[2,2,1,256,256]{4,1,3,2,0:T(2,128)S(1)}, f32[2,2,1,256,256]{4,1,3,2,0:T(2,128)S(1)}, u32[]{:S(2)}, u32[]{:S(2)}) collective-permute-start(f32[2,2,1,256,256]{4,1,3,2,0:T(2,128)S(1)} %pad_maximum_fusion.4), channel_id=1, source_target_pairs={{0,1},{1,2},{2,3},{3,4},{4,5},{5,6},{6,7},{7,8},{8,9},{9,10},{10,1... | collective-permute-start | bytes 3145736 | tf_op jit(solution)/shard_map/ppermute | solution.py:21
  111.7 1.9 copy-start
  139.4 18.4 %collective-permute-start.3 = (f32[2,2,1,256,256]{4,1,3,2,0:T(2,128)S(1)}, f32[2,2,1,256,256]{4,1,3,2,0:T(2,128)S(1)}, u32[]{:S(2)}, u32[]{:S(2)}) collective-permute-start(f32[2,2,1,256,256]{4,1,3,2,0:T(2,128)S(1)} %pad_maximum_fusion.5), channel_id=1, source_target_pairs={{1,0},{2,1},{3,2},{4,3},{5,4},{6,5},{7,6},{8,7},{9,8},{10,9},{11,1... | collective-permute-start | bytes 3145736 | tf_op jit(solution)/shard_map/ppermute | solution.py:23
  141.3 18.6 %collective-permute-start.2 = (f32[2,2,1,256,256]{4,1,3,2,0:T(2,128)S(1)}, f32[2,2,1,256,256]{4,1,3,2,0:T(2,128)S(1)}, u32[]{:S(2)}, u32[]{:S(2)}) collective-permute-start(f32[2,2,1,256,256]{4,1,3,2,0:T(2,128)S(1)} %pad_maximum_fusion.5), channel_id=1, source_target_pairs={{0,1},{1,2},{2,3},{3,4},{4,5},{5,6},{6,7},{7,8},{8,9},{9,10},{10,1... | collective-permute-start | bytes 3145736 | tf_op jit(solution)/shard_map/ppermute | solution.py:21
  168.3 18.4 %collective-permute-start.5 = (f32[2,2,1,256,256]{4,1,3,2,0:T(2,128)S(1)}, f32[2,2,1,256,256]{4,1,3,2,0:T(2,128)S(1)}, u32[]{:S(2)}, u32[]{:S(2)}) collective-permute-start(f32[2,2,1,256,256]{4,1,3,2,0:T(2,128)S(1)} %pad_maximum_fusion.6), channel_id=1, source_target_pairs={{1,0},{2,1},{3,2},{4,3},{5,4},{6,5},{7,6},{8,7},{9,8},{10,9},{11,1... | collective-permute-start | bytes 3145736 | tf_op jit(solution)/shard_map/ppermute | solution.py:23
  170.2 24.4 %collective-permute-start.4 = (f32[2,2,1,256,256]{4,1,3,2,0:T(2,128)S(1)}, f32[2,2,1,256,256]{4,1,3,2,0:T(2,128)S(1)}, u32[]{:S(2)}, u32[]{:S(2)}) collective-permute-start(f32[2,2,1,256,256]{4,1,3,2,0:T(2,128)S(1)} %pad_maximum_fusion.6), channel_id=1, source_target_pairs={{0,1},{1,2},{2,3},{3,4},{4,5},{5,6},{6,7},{7,8},{8,9},{9,10},{10,1... | collective-permute-start | bytes 3145736 | tf_op jit(solution)/shard_map/ppermute | solution.py:21
  203.0 18.4 %collective-permute-start.7 = (f32[2,2,1,256,256]{4,1,3,2,0:T(2,128)S(1)}, f32[2,2,1,256,256]{4,1,3,2,0:T(2,128)S(1)}, u32[]{:S(2)}, u32[]{:S(2)}) collective-permute-start(f32[2,2,1,256,256]{4,1,3,2,0:T(2,128)S(1)} %pad_maximum_fusion.7), channel_id=1, source_target_pairs={{1,0},{2,1},{3,2},{4,3},{5,4},{6,5},{7,6},{8,7},{9,8},{10,9},{11,1... | collective-permute-start | bytes 3145736 | tf_op jit(solution)/shard_map/ppermute | solution.py:23
  204.9 18.6 %collective-permute-start.6 = (f32[2,2,1,256,256]{4,1,3,2,0:T(2,128)S(1)}, f32[2,2,1,256,256]{4,1,3,2,0:T(2,128)S(1)}, u32[]{:S(2)}, u32[]{:S(2)}) collective-permute-start(f32[2,2,1,256,256]{4,1,3,2,0:T(2,128)S(1)} %pad_maximum_fusion.7), channel_id=1, source_target_pairs={{0,1},{1,2},{2,3},{3,4},{4,5},{5,6},{6,7},{7,8},{8,9},{9,10},{10,1... | collective-permute-start | bytes 3145736 | tf_op jit(solution)/shard_map/ppermute | solution.py:21
  230.2 12.0 %collective-permute-start.9 = (f32[2,1,256,256]{3,0,2,1:T(2,128)S(1)}, f32[2,1,256,256]{3,0,2,1:T(2,128)S(1)}, u32[]{:S(2)}, u32[]{:S(2)}) collective-permute-start(f32[2,1,256,256]{3,0,2,1:T(2,128)S(1)} %get-tuple-element.24), channel_id=1, source_target_pairs={{0,1},{1,2},{2,3},{3,4},{4,5},{5,6},{6,7},{7,8},{8,9},{9,10},{10,1... | collective-permute-start | bytes 1572872 | tf_op jit(solution)/shard_map/ppermute | solution.py:21
  236.1 12.0 %collective-permute-start.8 = (f32[2,1,256,256]{3,0,2,1:T(2,128)S(1)}, f32[2,1,256,256]{3,0,2,1:T(2,128)S(1)}, u32[]{:S(2)}, u32[]{:S(2)}) collective-permute-start(f32[2,1,256,256]{3,0,2,1:T(2,128)S(1)} %get-tuple-element.24), channel_id=1, source_target_pairs={{1,0},{2,1},{3,2},{4,3},{5,4},{6,5},{7,6},{8,7},{9,8},{10,9},{11,1... | collective-permute-start | bytes 1572872 | tf_op jit(solution)/shard_map/ppermute | solution.py:23
  251.4 10.9 %collective-permute-start.11 = (f32[2,1,256,256]{3,0,2,1:T(2,128)S(1)}, f32[2,1,256,256]{3,0,2,1:T(2,128)S(1)}, u32[]{:S(2)}, u32[]{:S(2)}) collective-permute-start(f32[2,1,256,256]{3,0,2,1:T(2,128)S(1)} %get-tuple-element.48), channel_id=1, source_target_pairs={{0,1},{1,2},{2,3},{3,4},{4,5},{5,6},{6,7},{7,8},{8,9},{9,10},{10,1... | collective-permute-start | bytes 1572872 | tf_op jit(solution)/shard_map/ppermute | solution.py:21
  253.4 17.0 %collective-permute-start.10 = (f32[2,1,256,256]{3,0,2,1:T(2,128)S(1)}, f32[2,1,256,256]{3,0,2,1:T(2,128)S(1)}, u32[]{:S(2)}, u32[]{:S(2)}) collective-permute-start(f32[2,1,256,256]{3,0,2,1:T(2,128)S(1)} %get-tuple-element.48), channel_id=1, source_target_pairs={{1,0},{2,1},{3,2},{4,3},{5,4},{6,5},{7,6},{8,7},{9,8},{10,9},{11,1... | collective-permute-start | bytes 1572872 | tf_op jit(solution)/shard_map/ppermute | solution.py:23
  273.7 10.6 %collective-permute-start.13 = (f32[2,1,256,256]{3,0,2,1:T(2,128)S(1)}, f32[2,1,256,256]{3,0,2,1:T(2,128)S(1)}, u32[]{:S(2)}, u32[]{:S(2)}) collective-permute-start(f32[2,1,256,256]{3,0,2,1:T(2,128)S(1)} %get-tuple-element.46), channel_id=1, source_target_pairs={{0,1},{1,2},{2,3},{3,4},{4,5},{5,6},{6,7},{7,8},{8,9},{9,10},{10,1... | collective-permute-start | bytes 1572872 | tf_op jit(solution)/shard_map/ppermute | solution.py:21
  275.6 12.9 %collective-permute-start.12 = (f32[2,1,256,256]{3,0,2,1:T(2,128)S(1)}, f32[2,1,256,256]{3,0,2,1:T(2,128)S(1)}, u32[]{:S(2)}, u32[]{:S(2)}) collective-permute-start(f32[2,1,256,256]{3,0,2,1:T(2,128)S(1)} %get-tuple-element.46), channel_id=1, source_target_pairs={{1,0},{2,1},{3,2},{4,3},{5,4},{6,5},{7,6},{8,7},{9,8},{10,9},{11,1... | collective-permute-start | bytes 1572872 | tf_op jit(solution)/shard_map/ppermute | solution.py:23
  291.8 10.7 %collective-permute-start.15 = (f32[2,1,256,256]{3,0,2,1:T(2,128)S(1)}, f32[2,1,256,256]{3,0,2,1:T(2,128)S(1)}, u32[]{:S(2)}, u32[]{:S(2)}) collective-permute-start(f32[2,1,256,256]{3,0,2,1:T(2,128)S(1)} %get-tuple-element.50), channel_id=1, source_target_pairs={{0,1},{1,2},{2,3},{3,4},{4,5},{5,6},{6,7},{7,8},{8,9},{9,10},{10,1... | collective-permute-start | bytes 1572872 | tf_op jit(solution)/shard_map/ppermute | solution.py:21
  293.8 12.9 %collective-permute-start.14 = (f32[2,1,256,256]{3,0,2,1:T(2,128)S(1)}, f32[2,1,256,256]{3,0,2,1:T(2,128)S(1)}, u32[]{:S(2)}, u32[]{:S(2)}) collective-permute-start(f32[2,1,256,256]{3,0,2,1:T(2,128)S(1)} %get-tuple-element.50), channel_id=1, source_target_pairs={{1,0},{2,1},{3,2},{4,3},{5,4},{6,5},{7,6},{8,7},{9,8},{10,9},{11,1... | collective-permute-start | bytes 1572872 | tf_op jit(solution)/shard_map/ppermute | solution.py:23
Sparse Core Ops, SparseCore 0:
  9.6 39.2 all-gather.2
  50.5 46.4 all-gather.4
  320.5 80.5 reduce-scatter.1
where the time goes:
time: 412 us; the launch traced here: 408 us
  waiting for transfers between devices  232 us (56%)
  starting transfers between devices  55.5 us (13%)
  other arithmetic  42.8 us (10%)
  local copies, waits for them, and re-layouts  32.5 us (8%)
  matrix products  30.4 us (7%)
  between operations  14.8 us (4%)
    reduce_scatter x1, waiting for transfers between devices, local(): lax.psum_scatter(partial_value, 'step', scatter_dimension=0, tiled=True)  79 us
    ppermute x8, waiting for transfers between devices, with_halo(): lax.ppermute(head, axis, [((i + 1) % count, i) for i in range(ends)])  46.3 us
    all_gather x1, waiting for transfers between devices, local(): piece = lax.all_gather(drift, 'step', axis=0, tiled=True)  43.3 us
    all_gather x1, waiting for transfers between devices, local(): gathered_snaps = lax.all_gather(snapshots, 'step', axis=0, tiled=True)  38.1 us
    ppermute x8, starting transfers between devices, with_halo(): lax.ppermute(tail, axis, [(i, (i + 1) % count) for i in range(ends)])  34.6 us
    ppermute x8, waiting for transfers between devices, with_halo(): lax.ppermute(tail, axis, [(i, (i + 1) % count) for i in range(ends)])  23.7 us
    ppermute x8, starting transfers between devices, with_halo(): lax.ppermute(head, axis, [((i + 1) % count, i) for i in range(ends)])  20.8 us
    dot_general x4, matrix products, local(): jnp.einsum('ps,pczyx->sczyx', onehot, term, precision=lax.Precision.HIGHEST)  20 us
  transfers between devices with their start and end apart: 19, of which 15 were waited for; matrix products, arithmetic and copies ran while one was open for 11% of the time, Pallas kernels for 0%

commit v1 on v0

v1 whole, which is shorter than its diff:
```python
import jax
import jax.numpy as jnp
from jax import lax
from jax.experimental import pallas as pl
from jax.experimental.pallas import tpu as pltpu
from jax.sharding import PartitionSpec as P

WIN = 4
NZ = 16
SIDE = 256
PAIRS = 16
STEPS = 8
OWN_Y = 32
OWN_X = 16
HALO = 2 * WIN
PITCH = OWN_X + 2 * HALO
GROUPS = (OWN_Y + 2 * HALO) // 4
OWN_LO = HALO // 4
OWN_HI = OWN_LO + OWN_Y // 4
IN_ROWS = 64
OUT_ROWS = 32
VREG = (8, 128)
TABLE_ROW = 60

time_step = 0.1
diffusion = 1.0
near = time_step * diffusion
keep = 1.0 - 6.0 * near
half = 0.5 * time_step


def lanes():
    return lax.broadcasted_iota(jnp.int32, VREG, 1)


def subs():
    return lax.broadcasted_iota(jnp.int32, VREG, 0)


def build_kernel(pairs_ref, plan_ref, snap_ref, drift_ref, out_ref, field_ref, wide_ref):
    for f in range(4):
        for h in range(2):
            cols = slice(128 * h, 128 * h + 128)
            plane = snap_ref[0, 0, :, cols] if f == 0 else drift_ref[0, f - 1, 0, :, cols].astype(jnp.float32)
            field_ref[f, h, 8:264, :] = plane
            field_ref[f, h, 0:8, :] = plane[248:256]
            field_ref[f, h, 264:288, :] = plane[0:24]
    lane = lax.broadcasted_iota(jnp.int32, (72, 128), 1)
    table = jnp.zeros(VREG, jnp.float32)
    for i in range(12):
        entry = pairs_ref[i // 2, i % 2] if i < 4 else plan_ref[(i - 4) // 4, (i - 4) % 4]
        table = jnp.where(lanes() == i, entry.astype(jnp.float32), table)
    upper = subs() < 4
    for bx in range(16):
        start = (OWN_X * bx - HALO) % SIDE
        side, offset = start // 128, start % 128
        for f in range(4):
            parts = []
            for j in range(4):
                shift = (PITCH * j - offset) % 128
                rows = pl.ds(j, 72, stride=4)
                part = pltpu.roll(field_ref[f, side, rows, :], shift, 1)
                if offset > 96:
                    other = pltpu.roll(field_ref[f, 1 - side, rows, :], shift, 1)
                    part = jnp.where(lane < PITCH * j + 128 - offset, part, other)
                parts.append(part)
            whole = jnp.where(
                lane < 64,
                jnp.where(lane < 32, parts[0], parts[1]),
                jnp.where(lane < 96, parts[2], parts[3]),
            )
            if f == 0:
                high = whole.astype(jnp.bfloat16).astype(jnp.float32)
                wide_ref[0] = high
                wide_ref[1] = whole - high
            else:
                wide_ref[f + 1] = whole
        for by in range(8):
            top = [wide_ref[f, 8 * by : 8 * by + 8, :] for f in range(5)]
            tail = [wide_ref[f, 8 * by + 8 : 8 * by + 16, :] for f in range(5)]
            ends = [
                jnp.where(upper, tail[0], pltpu.roll(tail[1], 4, 0)),
                jnp.where(upper, tail[2], pltpu.roll(tail[3], 4, 0)),
                jnp.where(upper, tail[4], table),
            ]
            out_ref[by * 16 + bx] = jnp.concatenate(top + ends, axis=0).astype(jnp.bfloat16)


def in_row(f, group):
    return 8 * f + group if group < 8 else 40 + 4 * f + group - 8


def window_kernel(in_ref, out_ref, rows_ref, snap_ref, drift_ref, rho_ref, lam_ref, grad_ref, table_ref):
    lane = lanes()
    sub = subs()
    zero = jnp.zeros(VREG, jnp.float32)
    first, last = sub == 0, sub == 7
    low, high = lane < 128 - PITCH, lane >= PITCH
    even = (lane % PITCH) < OWN_X

    def unpack(s, carry):
        for z in range(NZ):
            rows_ref[64 * z : 64 * z + 64, :] = in_ref[s * NZ + z].astype(jnp.float32)
        for zo in range(2):
            for g in range(GROUPS):
                parts = [rows_ref[pl.ds(512 * zo + in_row(f, g), 8, stride=64), :] for f in range(5)]
                snap_ref[s, zo * GROUPS + g] = parts[0] + parts[1]
                for c in range(3):
                    drift_ref[s, c, zo * GROUPS + g] = half * parts[2 + c]
        entries = jnp.where(sub == TABLE_ROW % 8, rows_ref[TABLE_ROW - 4 : TABLE_ROW + 4, :], 0.0)
        for part in range(2):
            weight = zero
            for i in range(6):
                weight = jnp.where(lane == 6 * part + i, float(8**i), weight)
            code = jnp.sum(entries * weight).astype(jnp.int32)
            for i in range(6):
                table_ref[s * 12 + 6 * part + i] = (code >> (3 * i)) & 7
        return carry

    lax.fori_loop(0, STEPS, unpack, 0)
    for i in range(STEPS * 3):
        for v in range(2 * (OWN_HI - OWN_LO)):
            grad_ref[i, v] = zero

    def next_z(a, b):
        u, w = pltpu.roll(a, 7, 0), pltpu.roll(b, 7, 0)
        return jnp.where(last, w, u), jnp.where(last, zero, w)

    def prev_z(a, b):
        u, w = pltpu.roll(a, 1, 0), pltpu.roll(b, 1, 0)
        return jnp.where(first, zero, u), jnp.where(first, u, w)

    def put(vectors, row):
        for zo in range(2):
            for gg in range(4):
                value = jnp.where(
                    even,
                    pltpu.roll(vectors[zo, 2 * gg], 128 - HALO, 1),
                    pltpu.roll(vectors[zo, 2 * gg + 1], HALO, 1),
                )
                out_ref[pl.ds(row + 8 * OUT_ROWS * zo + gg, 8, stride=OUT_ROWS), :] = value

    def one_pair(p, carry):
        owner = p // 2
        base = owner * 12
        one = p % 2
        start = table_ref[base + 2 * one]
        target = table_ref[base + 2 * one + 1]
        steps = [table_ref[base + 4 + 4 * one + k] for k in range(WIN)]
        out_row = owner * (NZ * OUT_ROWS) + 4 * one

        def state(k, i):
            return snap_ref[start, i] if k == 0 else rho_ref[k - 1, i]

        for k in range(WIN):
            step = steps[k]
            lo, hi = (0, GROUPS) if k < WIN - 1 else (1, GROUPS - 1)
            mids, ups, downs = {}, {}, {}
            finals = {}
            for g in range(GROUPS + 1):
                if g < GROUPS:
                    wp, wm, mid = [], [], []
                    for zo in range(2):
                        i = zo * GROUPS + g
                        rho = state(k, i)
                        spread = near * rho
                        hx = drift_ref[step, 0, i] * rho
                        hy = drift_ref[step, 1, i] * rho
                        hz = drift_ref[step, 2, i] * rho
                        downs[zo, g] = pltpu.roll(spread - hy, 128 - PITCH, 1)
                        ups[zo, g] = pltpu.roll(spread + hy, PITCH, 1)
                        mid.append(keep * rho + pltpu.roll(spread - hx, 127, 1) + pltpu.roll(spread + hx, 1, 1))
                        wp.append(spread + hz)
                        wm.append(spread - hz)
                    n = next_z(*wm)
                    q = prev_z(*wp)
                    for zo in range(2):
                        mids[zo, g] = mid[zo] + n[zo] + q[zo]
                d = g - 1
                if d >= lo and d < hi:
                    for zo in range(2):
                        after = downs[zo, min(d + 1, GROUPS - 1)]
                        before = ups[zo, max(d - 1, 0)]
                        value = mids[zo, d] + jnp.where(low, downs[zo, d], after) + jnp.where(high, ups[zo, d], before)
                        i = zo * GROUPS + d
                        if k < WIN - 1:
                            rho_ref[k, i] = value
                        else:
                            lam_ref[0, i] = value - snap_ref[target, i]
                            finals[zo, d - OWN_LO] = value
            if k == WIN - 1:
                put(finals, out_row)

        for index in range(WIN):
            k = WIN - 1 - index
            step = steps[k]
            source, sink = index % 2, 1 - index % 2
            lo, hi = (1, GROUPS - 1) if index < WIN - 1 else (OWN_LO, OWN_HI)
            fields, ups, downs = {}, {}, {}
            finals = {}
            for g in range(1, GROUPS):
                if g < GROUPS - 1:
                    for zo in range(2):
                        lam = lam_ref[source, zo * GROUPS + g]
                        fields[zo, g] = lam
                        downs[zo, g] = pltpu.roll(lam, 128 - PITCH, 1)
                        ups[zo, g] = pltpu.roll(lam, PITCH, 1)
                d = g - 1
                if d >= lo and d < hi:
                    n = next_z(fields[0, d], fields[1, d])
                    q = prev_z(fields[0, d], fields[1, d])
                    for zo in range(2):
                        i = zo * GROUPS + d
                        lam = fields[zo, d]
                        xp, xm = pltpu.roll(lam, 127, 1), pltpu.roll(lam, 1, 1)
                        yp = jnp.where(low, downs[zo, d], downs[zo, min(d + 1, GROUPS - 2)])
                        ym = jnp.where(high, ups[zo, d], ups[zo, max(d - 1, 1)])
                        dx, dy, dz = xp - xm, yp - ym, n[zo] - q[zo]
                        total = (xp + xm) + (yp + ym) + (n[zo] + q[zo])
                        value = (
                            keep * lam
                            + near * total
                            + drift_ref[step, 0, i] * dx
                            + drift_ref[step, 1, i] * dy
                            + drift_ref[step, 2, i] * dz
                        )
                        if index < WIN - 1:
                            lam_ref[sink, i] = value
                        else:
                            finals[zo, d - OWN_LO] = value
                        if OWN_LO <= d < OWN_HI:
                            weight = half * state(k, i)
                            v = zo * (OWN_HI - OWN_LO) + d - OWN_LO
                            for c, slope in enumerate((dx, dy, dz)):
                                grad_ref[step * 3 + c, v] += weight * slope
            if index == WIN - 1:
                put(finals, out_row + 8)
        return carry

    lax.fori_loop(0, PAIRS, one_pair, 0)

    def store_grads(s, carry):
        for c in range(3):
            own = {
                (zo, g): grad_ref[s * 3 + c, zo * (OWN_HI - OWN_LO) + g]
                for zo in range(2)
                for g in range(OWN_HI - OWN_LO)
            }
            put(own, s * (NZ * OUT_ROWS) + 16 + 4 * c)
        return carry

    lax.fori_loop(0, STEPS, store_grads, 0)


def planes_kernel(in_ref, final_ref, adjoint_ref, grad_ref, plane_ref):
    block = lanes() // OWN_X

    def rows_of(by, carry):
        for t in range(4):
            for h in range(2):
                v = [in_ref[by * 16 + 8 * h + a, 8 * t : 8 * t + 8, :] for a in range(8)]
                for bit in (1, 2, 4):
                    clear = (block & bit) == 0
                    for a in range(8):
                        if not a & bit:
                            u, w = v[a], v[a | bit]
                            v[a] = jnp.where(clear, u, pltpu.roll(w, 16 * bit, 1))
                            v[a | bit] = jnp.where(clear, pltpu.roll(u, 128 - 16 * bit, 1), w)
                for q in range(8):
                    row = 4 * (q % 2) + q // 2
                    plane_ref[2 * t, h, pl.ds(row, 4, stride=8), :] = v[q][0:4]
                    if t < 3:
                        plane_ref[2 * t + 1, h, pl.ds(row, 4, stride=8), :] = v[q][4:8]
        at = pl.multiple_of(by * OWN_Y, OWN_Y)
        for h in range(2):
            cols = slice(128 * h, 128 * h + 128)
            for i in range(2):
                final_ref[i, 0, pl.ds(at, OWN_Y), cols] = plane_ref[i, h]
                adjoint_ref[i, 0, pl.ds(at, OWN_Y), cols] = plane_ref[2 + i, h]
            for c in range(3):
                grad_ref[0, c, 0, pl.ds(at, OWN_Y), cols] = plane_ref[4 + c, h]
        return carry

    lax.fori_loop(0, 8, rows_of, 0)


def local(snapshots, drift, pair_table, plan):
    f32, bf16 = jnp.float32, jnp.bfloat16
    smem = pl.BlockSpec(memory_space=pltpu.SMEM)
    vmem = pl.BlockSpec(memory_space=pltpu.VMEM)
    windows = pl.pallas_call(
        build_kernel,
        out_shape=jax.ShapeDtypeStruct((128, IN_ROWS, 128), bf16),
        in_specs=[smem, smem, vmem, vmem],
        out_specs=vmem,
        scratch_shapes=[pltpu.VMEM((4, 2, 288, 128), f32), pltpu.VMEM((5, 72, 128), f32)],
    )(pair_table, plan, snapshots, drift)
    windows = lax.all_to_all(windows, ("step", "space"), 0, 0, tiled=True)
    groups = 2 * GROUPS
    results = pl.pallas_call(
        window_kernel,
        out_shape=jax.ShapeDtypeStruct((128 * OUT_ROWS, 128), f32),
        in_specs=[vmem],
        out_specs=vmem,
        scratch_shapes=[
            pltpu.VMEM((NZ * IN_ROWS, 128), f32),
            pltpu.VMEM((STEPS, groups) + VREG, f32),
            pltpu.VMEM((STEPS, 3, groups) + VREG, f32),
            pltpu.VMEM((WIN - 1, groups) + VREG, f32),
            pltpu.VMEM((2, groups) + VREG, f32),
            pltpu.VMEM((STEPS * 3, 2 * (OWN_HI - OWN_LO)) + VREG, f32),
            pltpu.SMEM((STEPS * 12,), jnp.int32),
        ],
    )(windows)
    results = results.reshape(128, OUT_ROWS, 128)
    results = lax.all_to_all(results, ("step", "space"), 0, 0, tiled=True)
    return pl.pallas_call(
        planes_kernel,
        out_shape=(
            jax.ShapeDtypeStruct((2, 1, SIDE, SIDE), f32),
            jax.ShapeDtypeStruct((2, 1, SIDE, SIDE), f32),
            jax.ShapeDtypeStruct((1, 3, 1, SIDE, SIDE), f32),
        ),
        in_specs=[vmem],
        out_specs=(vmem, vmem, vmem),
        scratch_shapes=[pltpu.VMEM((7, 2, OWN_Y, 128), f32)],
    )(results)


def solution(mesh):
    return jax.shard_map(
        local,
        mesh=mesh,
        in_specs=(
            P("step", "space", None, None),
            P("step", None, "space", None, None),
            P("step", None),
            P("step", None),
        ),
        out_specs=(
            P("step", "space", None, None),
            P("step", "space", None, None),
            P("step", None, "space", None, None),
        ),
        check_vma=False,
    )
```

time: 412 us -> 111 us (0.27)
  waiting for transfers between devices: 232 us -> 0 us
  blocking collectives: 0 us -> 76.6 us
  starting transfers between devices: 55.5 us -> 0 us
  other arithmetic: 42.8 us -> 0 us
  Pallas kernels: 0 us -> 33.3 us
  local copies, waits for them, and re-layouts: 32.5 us -> 0 us
  matrix products: 30.4 us -> 0 us
  between operations: 14.8 us -> 0.63 us
    all_gather x2 -> x0, waiting for transfers between devices: 81.5 us -> none  [the longest x1 43.3 us: local(): piece = lax.all_gather(drift, 'step', axis=0, tiled=True)]
    reduce_scatter x1 -> x0, waiting for transfers between devices: 79 us -> none  [local(): lax.psum_scatter(partial_value, 'step', scatter_dimension=0, tiled=True)]
    all_to_all x0 -> x2, blocking collectives: none -> 76.6 us  [the longest x1 41.8 us: local(): windows = lax.all_to_all(windows, ('step', 'space'), 0, 0, tiled=True)]
    ppermute x16 -> x0, waiting for transfers between devices: 70.1 us -> none  [the longest x8 46.3 us: with_halo(): lax.ppermute(head, axis, [((i + 1) % count, i) for i in range(ends)])]
    ppermute x16 -> x0, starting transfers between devices: 55.4 us -> none  [the longest x8 34.6 us: with_halo(): lax.ppermute(tail, axis, [(i, (i + 1) % count) for i in range(ends)])]
    pallas_call x0 -> x3, Pallas kernels: none -> 33.3 us  [the longest x1 23.1 us: local(): pl.pallas_call(window_kernel, out_shape=jax.ShapeDtypeStruct((128 * OUT_R...]
    dot_general x8 -> x0, matrix products: 30.4 us -> none  [the longest x4 20 us: local(): jnp.einsum('ps,pczyx->sczyx', onehot, term, precision=lax.Precision.HIGHEST)]
    mul x16 -> x0, other arithmetic: 29.2 us -> none  [the longest x8 13.6 us: diff_plane(): return (jnp.roll(field, -1, axis) - jnp.roll(field, 1, axis)) * 0.5]
  transfers between devices with their start and end apart: 19 -> 0, of which waited for: 15 -> 0; matrix products, arithmetic and copies ran while one was open for 11% -> 0% of each run, Pallas kernels for 0% -> 0%
where the time goes in v1:
time: 111 us
  blocking collectives  76.6 us (69%)
  Pallas kernels  33.3 us (30%)
    all_to_all x1, blocking collectives, local(): windows = lax.all_to_all(windows, ('step', 'space'), 0, 0, tiled=True)  41.8 us
    all_to_all x1, blocking collectives, local(): results = lax.all_to_all(results, ('step', 'space'), 0, 0, tiled=True)  34.8 us
    pallas_call x1, Pallas kernels, local(): pl.pallas_call(window_kernel, out_shape=jax.ShapeDtypeStruct((128 * OUT_R...  23.1 us
    pallas_call x1, Pallas kernels, local(): pl.pallas_call(planes_kernel, out_shape=(jax.ShapeDtypeStruct((2, 1, SIDE...  5.79 us
    pallas_call x1, Pallas kernels, local(): pl.pallas_call(build_kernel, out_shape=jax.ShapeDtypeStruct((128, IN_ROWS...  4.39 us

profile of v1, /device:TPU:1, one launch (start us, length us, event | category | flops | bytes accessed | tf_op | source)
XLA Modules:
  0.0 110.5 jit_solution(10849754132102502957)
XLA Ops:
  0.6 4.4 %shard_map.67 = bf16[128,64,128]{2,1,0:T(8,128)(2,1)} custom-call(s32[2,2]{1,0:T(2,128)} %pairs_ref.1, s32[2,4]{1,0:T(2,128)} %plan_ref.1, f32[1,1,256,256]{3,2,1,0:T(8,128)} %snap_ref.1, bf16[1,3,1,256,256]{4,3,2,1,0:T(8,128)(2,1)} %drift_ref.1), custom_call_target="tpu_custom_call" | custom-call | tf_op jit(solution)/shard_map/pallas_call | solution.py:291
  5.0 41.8 %all_to_all.10.in_ref = bf16[128,64,128]{2,1,0:T(8,128)(2,1)} all-to-all(bf16[128,64,128]{2,1,0:T(8,128)(2,1)} %shard_map.67), channel_id=1, replica_groups=mesh['step'=8,'space'=16] {'step','space'}, dimensions={0} | all-to-all | bytes 4194304 | tf_op jit(solution)/shard_map/all_to_all | solution.py:298
  46.8 23.1 %shard_map.68 = f32[4096,128]{1,0:T(8,128)} custom-call(bf16[128,64,128]{2,1,0:T(8,128)(2,1)} %all_to_all.10.in_ref), custom_call_target="tpu_custom_call" | custom-call | tf_op jit(solution)/shard_map/pallas_call | solution.py:300
  69.9 34.8 %all_to_all.11.in_ref = f32[128,32,128]{2,1,0:T(8,128)} all-to-all(f32[128,32,128]{2,1,0:T(8,128)} %bitcast.1), channel_id=1, replica_groups=mesh['step'=8,'space'=16] {'step','space'}, dimensions={0} | all-to-all | bytes 4194304 | tf_op jit(solution)/shard_map/all_to_all | solution.py:316
  104.7 5.8 %shard_map.69 = (f32[2,1,256,256]{3,2,1,0:T(8,128)}, f32[2,1,256,256]{3,2,1,0:T(8,128)}, f32[1,3,1,256,256]{4,3,2,1,0:T(8,128)}) custom-call(f32[128,32,128]{2,1,0:T(8,128)} %all_to_all.11.in_ref), custom_call_target="tpu_custom_call" | custom-call | tf_op jit(solution)/shard_map/pallas_call | solution.py:317

commit v2 on v1

v2 whole, which is shorter than its diff:
```python
import jax
import jax.numpy as jnp
from jax import lax
from jax.experimental import pallas as pl
from jax.experimental.pallas import tpu as pltpu
from jax.sharding import PartitionSpec as P

WIN = 4
NZ = 16
SIDE = 256
PAIRS = 16
STEPS = 8
OWN_Y = 32
OWN_X = 16
HALO = 2 * WIN
PITCH = OWN_X + 2 * HALO
OWN = 8
GROUPS = 12
IN_ROWS = 64
OUT_ROWS = 28
VREG = (8, 128)

time_step = 0.1
diffusion = 1.0
near = time_step * diffusion
keep = 1.0 - 6.0 * near
half = 0.5 * time_step


def lanes():
    return lax.broadcasted_iota(jnp.int32, VREG, 1)


def subs():
    return lax.broadcasted_iota(jnp.int32, VREG, 0)


def spread_of(sign):
    return jnp.exp2(((lanes() * 37) % 128).astype(jnp.float32) * (sign / 128.0))


def swap(u, w, clear, width):
    return jnp.where(clear, u, pltpu.roll(w, width, 1)), jnp.where(clear, pltpu.roll(u, 128 - width, 1), w)


def build_kernel(pairs_ref, plan_ref, snap_ref, drift_ref, out_ref, tile_ref):
    lane = lanes()
    block = lane // PITCH
    one, two = (block & 1) == 0, (block & 2) == 0
    wrap = lane < 112
    outer = (block == 0) | (block == 3)
    table = jnp.zeros(VREG, jnp.float32)
    for i in range(12):
        entry = pairs_ref[i // 2, i % 2] if i < 4 else plan_ref[(i - 4) // 4, (i - 4) % 4]
        table = jnp.where(lane == PITCH + i, entry.astype(jnp.float32), table)

    def tiles(by, carry):
        at = pl.multiple_of(32 * by, 32)
        for f in range(4):
            even, odd = {}, {}
            for j in range(4):
                rows = pl.ds(at + 8 * j, 8)
                if f == 0:
                    parts = [snap_ref[0, 0, rows, 128 * h : 128 * h + 128] for h in range(2)]
                else:
                    parts = [
                        drift_ref[0, f - 1, 0, rows, 128 * h : 128 * h + 128].astype(jnp.float32) for h in range(2)
                    ]
                moved = [pltpu.roll(part, 112, 1) for part in parts]
                for h in range(2):
                    even[h, j] = parts[h]
                    odd[h, j] = jnp.where(wrap, moved[h], moved[1 - h])
            for h in range(2):
                for parity, source in enumerate((even, odd)):
                    v = [source[h, j] for j in range(4)]
                    v[0], v[1] = swap(v[0], v[1], one, PITCH)
                    v[2], v[3] = swap(v[2], v[3], one, PITCH)
                    v[0], v[2] = swap(v[0], v[2], two, 2 * PITCH)
                    v[1], v[3] = swap(v[1], v[3], two, 2 * PITCH)
                    for b in range(4):
                        bx = 8 * h + 2 * b + parity
                        tile_ref[f, bx, pl.ds(pl.multiple_of(8 * by, 8), 8), :] = v[b]
        return carry

    lax.fori_loop(0, 8, tiles, 0)

    def messages(bx, carry):
        for by in range(8):
            own, rim = [], []
            for f in range(4):
                tile = tile_ref[f, bx, 8 * by : 8 * by + 8, :]
                below = (8 * by + 8) % 64
                above = (8 * by - 8) % 64
                edge = jnp.where(
                    block == 0, tile_ref[f, bx, below : below + 8, :], tile_ref[f, bx, above : above + 8, :]
                )
                if f == 0:
                    for values, value in ((own, tile), (rim, edge)):
                        high = value.astype(jnp.bfloat16).astype(jnp.float32)
                        values += [high, value - high]
                else:
                    own.append(tile)
                    rim.append(edge)
            ends = [
                jnp.where(outer, rim[0], pltpu.roll(rim[1], 64, 1)),
                jnp.where(outer, rim[2], pltpu.roll(rim[3], 64, 1)),
                jnp.where(outer, rim[4], table),
            ]
            out_ref[by * 16 + bx] = jnp.concatenate(own + ends, axis=0).astype(jnp.bfloat16)
        return carry

    lax.fori_loop(0, 16, messages, 0)


PLANE_ROWS = 65


def window_kernel(in_ref, out_ref, rows_ref, snap_ref, drift_ref, rho_ref, lam_ref, grad_ref, table_ref):
    lane = lanes()
    sub = subs()
    zero = jnp.zeros(VREG, jnp.float32)
    first, last = sub == 0, sub == 7
    block = lane // PITCH
    is0, is3 = block == 0, block == 3
    outer = is0 | is3
    mine = (lane % PITCH >= HALO) & (lane % PITCH < HALO + OWN_X)

    def unpack(s, carry):
        for z in range(NZ):
            rows_ref[PLANE_ROWS * z : PLANE_ROWS * z + IN_ROWS, :] = in_ref[s * NZ + z].astype(jnp.float32)
        for zo in range(2):

            def row(r):
                return rows_ref[pl.ds(PLANE_ROWS * zo + r, 8, stride=2 * PLANE_ROWS), :]

            for g in range(GROUPS):
                if g < OWN:
                    parts = [row(8 * f + g) for f in range(5)]
                else:
                    e = g - OWN
                    parts = []
                    for t in range(3):
                        a, b = row(40 + 8 * t + e), row(44 + 8 * t + e)
                        direct, across = jnp.where(is0, a, b), jnp.where(is0, b, a)
                        parts.append(jnp.where(outer, direct, pltpu.roll(across, 64, 1)))
                        if t < 2:
                            direct, across = jnp.where(block == 1, a, b), jnp.where(block == 1, b, a)
                            parts.append(jnp.where(outer, pltpu.roll(across, 64, 1), direct))
                snap_ref[s, zo * GROUPS + g] = parts[0] + parts[1]
                for c in range(3):
                    drift_ref[s, c, zo * GROUPS + g] = near + half * parts[2 + c]
        entries = rows_ref[56:57, :]
        at = lax.broadcasted_iota(jnp.int32, (1, 128), 1) - PITCH
        for part in range(2):
            weight = jnp.zeros((1, 128), jnp.float32)
            for i in range(6):
                weight = jnp.where(at == 6 * part + i, float(8**i), weight)
            code = jnp.sum(entries * weight).astype(jnp.int32)
            for i in range(6):
                table_ref[s * 12 + 6 * part + i] = (code >> (3 * i)) & 7
        return carry

    lax.fori_loop(0, STEPS, unpack, 0)

    def clear(i, carry):
        for v in range(2 * OWN):
            grad_ref[i, v] = zero
        return carry

    lax.fori_loop(0, STEPS * 3, clear, 0)

    scale = spread_of(1.0)

    def put(vectors, row, factor):
        for zo in range(2):
            for gg in range(4):
                value = jnp.where(mine, vectors[zo, 2 * gg], pltpu.roll(vectors[zo, 2 * gg + 1], OWN_X, 1))
                out_ref[pl.ds(row + OUT_ROWS * zo + gg, 8, stride=2 * OUT_ROWS), :] = value * factor

    def from_below(g, zo, v):
        if g == 7:
            return pltpu.roll(jnp.where(is0, v[zo, 8], v[zo, 0]), 96, 1)
        if g == 11:
            return jnp.where(is3, pltpu.roll(v[zo, 0], 96, 1), pltpu.roll(v[zo, 8], 64, 1))
        return v[zo, g + 1]

    def from_above(g, zo, v):
        if g == 0:
            return pltpu.roll(jnp.where(is3, v[zo, 11], v[zo, 7]), 32, 1)
        if g == 8:
            return jnp.where(is0, pltpu.roll(v[zo, 7], 32, 1), pltpu.roll(v[zo, 11], 64, 1))
        return v[zo, g - 1]

    needs = {g: {g, g + 1, g - 1} for g in range(GROUPS)}
    needs[0] = {0, 1, 7, 11}
    needs[7] = {7, 6, 0, 8}
    needs[8] = {8, 9, 7, 11}
    needs[11] = {11, 10, 0, 8}
    order = (7, 11, 8, 0, 1, 2, 3, 4, 5, 6, 9, 10)

    def one_pair(p, carry):
        owner = p // 2
        base = owner * 12
        which = p % 2
        start = table_ref[base + 2 * which]
        target = table_ref[base + 2 * which + 1]
        steps = [table_ref[base + 4 + 4 * which + k] for k in range(WIN)]
        out_row = owner * (NZ * OUT_ROWS) + 4 * which

        def state(k, i):
            return snap_ref[start, i] if k == 0 else rho_ref[k - 1, i]

        for k in range(WIN):
            step = steps[k]
            mids, ups, downs, finals = {}, {}, {}, {}
            done, todo = set(), list(order)
            for g in order:
                zp, zm = [], []
                for zo in range(2):
                    i = zo * GROUPS + g
                    rho = state(k, i)
                    both = (2.0 * near) * rho
                    xp = drift_ref[step, 0, i] * rho
                    yp = drift_ref[step, 1, i] * rho
                    zp.append(drift_ref[step, 2, i] * rho)
                    zm.append(both - zp[zo])
                    downs[zo, g] = both - yp
                    ups[zo, g] = yp
                    mids[zo, g] = keep * rho + (pltpu.roll(both - xp, 127, 1) + pltpu.roll(xp, 1, 1))
                mids[0, g] += zm[1] + jnp.where(first, zero, pltpu.roll(zp[1], 1, 0))
                mids[1, g] += zp[0] + jnp.where(last, zero, pltpu.roll(zm[0], 7, 0))
                done.add(g)
                for d in [d for d in todo if needs[d] & set(order) <= done]:
                    todo.remove(d)
                    for zo in range(2):
                        value = mids[zo, d] + (from_below(d, zo, downs) + from_above(d, zo, ups))
                        i = zo * GROUPS + d
                        if k < WIN - 1:
                            rho_ref[k, i] = value
                        else:
                            lam_ref[0, i] = value - snap_ref[target, i]
                            finals[zo, d] = value
            if k == WIN - 1:
                put(finals, out_row, scale)

        for index in range(WIN):
            k = WIN - 1 - index
            step = steps[k]
            source, sink = index % 2, 1 - index % 2
            wanted = [g for g in order if g < OWN or index < 2 or (index == 2 and g in (8, 11))]
            fields, finals = {}, {}
            done, todo = set(), list(wanted)
            for g in [g for g in order if index < 3 or g not in (9, 10)]:
                for zo in range(2):
                    fields[zo, g] = lam_ref[source, zo * GROUPS + g]
                done.add(g)
                for d in [d for d in todo if needs[d] & set(order) <= done]:
                    todo.remove(d)
                    zn = fields[1, d], jnp.where(last, zero, pltpu.roll(fields[0, d], 7, 0))
                    zq = jnp.where(first, zero, pltpu.roll(fields[1, d], 1, 0)), fields[0, d]
                    for zo in range(2):
                        i = zo * GROUPS + d
                        lam = fields[zo, d]
                        xn, xq = pltpu.roll(lam, 127, 1), pltpu.roll(lam, 1, 1)
                        yn, yq = from_below(d, zo, fields), from_above(d, zo, fields)
                        dx, dy, dz = xn - xq, yn - yq, zn[zo] - zq[zo]
                        value = (
                            (keep * lam + (2.0 * near) * (xq + yq + zq[zo]))
                            + (drift_ref[step, 0, i] * dx + drift_ref[step, 1, i] * dy)
                            + drift_ref[step, 2, i] * dz
                        )
                        if index < WIN - 1:
                            lam_ref[sink, i] = value
                        else:
                            finals[zo, d] = value
                        if d < OWN:
                            rho = state(k, i)
                            for c, slope in enumerate((dx, dy, dz)):
                                grad_ref[step * 3 + c, zo * OWN + d] += rho * slope
            if index == WIN - 1:
                put(finals, out_row + 8, scale)
        return carry

    lax.fori_loop(0, PAIRS, one_pair, 0)

    def store_grads(s, carry):
        for c in range(3):
            own = {(zo, g): grad_ref[s * 3 + c, zo * OWN + g] for zo in range(2) for g in range(OWN)}
            put(own, s * (NZ * OUT_ROWS) + 16 + 4 * c, half * scale)
        return carry

    lax.fori_loop(0, STEPS, store_grads, 0)


def planes_kernel(in_ref, final_ref, adjoint_ref, grad_ref, plane_ref):
    lane = lanes()
    block = ((lane + 120) % 128) // OWN_X
    clear = {bit: (block & bit) == 0 for bit in (1, 2, 4)}
    inverse = spread_of(-1.0)
    carried = lane < HALO

    def rows_of(by, carry):
        for t in range(4):
            start = 8 * t if t < 3 else 20
            sides = []
            for h in range(2):
                v = [in_ref[pl.ds((by * 16 + 8 * h + a) * OUT_ROWS + start, 8), :] * inverse for a in range(8)]
                for bit in (1, 2, 4):
                    for a in range(8):
                        if not a & bit:
                            v[a], v[a | bit] = swap(v[a], v[a | bit], clear[bit], OWN_X * bit)
                sides.append(v)
            for h in range(2):
                for q in range(8):
                    value = jnp.where(carried, sides[1 - h][q], sides[h][q])
                    rows = pl.ds(8 * (q // 2) + q % 2, 4, stride=2)
                    if t < 3:
                        plane_ref[2 * t, h, rows, :] = value[0:4]
                        plane_ref[2 * t + 1, h, rows, :] = value[4:8]
                    else:
                        plane_ref[6, h, rows, :] = value[4:8]
        at = pl.multiple_of(by * OWN_Y, OWN_Y)
        for h in range(2):
            cols = slice(128 * h, 128 * h + 128)
            for i in range(2):
                final_ref[i, 0, pl.ds(at, OWN_Y), cols] = plane_ref[i, h]
                adjoint_ref[i, 0, pl.ds(at, OWN_Y), cols] = plane_ref[2 + i, h]
            for c in range(3):
                grad_ref[0, c, 0, pl.ds(at, OWN_Y), cols] = plane_ref[4 + c, h]
        return carry

    lax.fori_loop(0, 8, rows_of, 0)


def local(snapshots, drift, pair_table, plan):
    f32, bf16, f16 = jnp.float32, jnp.bfloat16, jnp.float16
    smem = pl.BlockSpec(memory_space=pltpu.SMEM)
    vmem = pl.BlockSpec(memory_space=pltpu.VMEM)
    windows = pl.pallas_call(
        build_kernel,
        out_shape=jax.ShapeDtypeStruct((128, IN_ROWS, 128), bf16),
        in_specs=[smem, smem, vmem, vmem],
        out_specs=vmem,
        scratch_shapes=[pltpu.VMEM((4, 16, 64, 128), f32)],
    )(pair_table, plan, snapshots, drift)
    windows = lax.all_to_all(windows, ("step", "space"), 0, 0, tiled=True)
    groups = 2 * GROUPS
    results = pl.pallas_call(
        window_kernel,
        out_shape=jax.ShapeDtypeStruct((128 * OUT_ROWS, 128), f32),
        in_specs=[vmem],
        out_specs=vmem,
        scratch_shapes=[
            pltpu.VMEM((NZ * PLANE_ROWS, 128), f32),
            pltpu.VMEM((STEPS, groups) + VREG, f32),
            pltpu.VMEM((STEPS, 3, groups) + VREG, f32),
            pltpu.VMEM((WIN - 1, groups) + VREG, f32),
            pltpu.VMEM((2, groups) + VREG, f32),
            pltpu.VMEM((STEPS * 3, 2 * OWN) + VREG, f32),
            pltpu.SMEM((STEPS * 12,), jnp.int32),
        ],
    )(windows)
    results = results.reshape(128, OUT_ROWS // 4, 4, 128).astype(f16)
    results = lax.all_to_all(results, ("step", "space"), 0, 0, tiled=True)
    results = results.astype(f32).reshape(128 * OUT_ROWS, 128)
    return pl.pallas_call(
        planes_kernel,
        out_shape=(
            jax.ShapeDtypeStruct((2, 1, SIDE, SIDE), f32),
            jax.ShapeDtypeStruct((2, 1, SIDE, SIDE), f32),
            jax.ShapeDtypeStruct((1, 3, 1, SIDE, SIDE), f32),
        ),
        in_specs=[vmem],
        out_specs=(vmem, vmem, vmem),
        scratch_shapes=[pltpu.VMEM((7, 2, OWN_Y, 128), f32)],
    )(results)


def solution(mesh):
    return jax.shard_map(
        local,
        mesh=mesh,
        in_specs=(
            P("step", "space", None, None),
            P("step", None, "space", None, None),
            P("step", None),
            P("step", None),
        ),
        out_specs=(
            P("step", "space", None, None),
            P("step", "space", None, None),
            P("step", None, "space", None, None),
        ),
        check_vma=False,
    )
```

time: 111 us -> 101 us (0.910)
  blocking collectives: 76.6 us -> 63.7 us
  other arithmetic: 0 us -> 2.99 us
    all_to_all x1, blocking collectives: 34.8 us -> 22 us  [local(): results = lax.all_to_all(results, ('step', 'space'), 0, 0, tiled=True)]
    convert_element_type x0 -> x1, other arithmetic: none -> 1.62 us  [local(): results = results.reshape(128, OUT_ROWS // 4, 4, 128).astype(f16)]
    pallas_call x1, Pallas kernels: 23.1 us -> 21.6 us  [local(): pl.pallas_call(window_kernel, out_shape=jax.ShapeDtypeStruct((128 * OUT_R...]
    pallas_call x1, Pallas kernels: 4.39 us -> 5.76 us  [local(): pl.pallas_call(build_kernel, out_shape=jax.ShapeDtypeStruct((128, IN_ROWS...]
    reshape x0 -> x1, other arithmetic: none -> 1.37 us  [local(): results = results.astype(f32).reshape(128 * OUT_ROWS, 128)]
where the time goes in v2:
time: 101 us
  blocking collectives  63.7 us (63%)
  Pallas kernels  33.2 us (33%)
  other arithmetic  2.99 us (3%)
    all_to_all x1, blocking collectives, local(): windows = lax.all_to_all(windows, ('step', 'space'), 0, 0, tiled=True)  41.8 us
    all_to_all x1, blocking collectives, local(): results = lax.all_to_all(results, ('step', 'space'), 0, 0, tiled=True)  22 us
    pallas_call x1, Pallas kernels, local(): pl.pallas_call(window_kernel, out_shape=jax.ShapeDtypeStruct((128 * OUT_R...  21.6 us
    pallas_call x1, Pallas kernels, local(): pl.pallas_call(build_kernel, out_shape=jax.ShapeDtypeStruct((128, IN_ROWS...  5.76 us
    pallas_call x1, Pallas kernels, local(): pl.pallas_call(planes_kernel, out_shape=(jax.ShapeDtypeStruct((2, 1, SIDE...  5.75 us

profile of v2, /device:TPU:1, one launch (start us, length us, event | category | flops | bytes accessed | tf_op | source)
XLA Modules:
  0.0 100.5 jit_solution(17104202038945985264)
XLA Ops:
  0.6 5.8 %shard_map.67 = bf16[128,64,128]{2,1,0:T(8,128)(2,1)} custom-call(s32[2,2]{1,0:T(2,128)} %pairs_ref.1, s32[2,4]{1,0:T(2,128)} %plan_ref.1, f32[1,1,256,256]{3,2,1,0:T(8,128)} %snap_ref.1, bf16[1,3,1,256,256]{4,3,2,1,0:T(8,128)(2,1)} %drift_ref.1), custom_call_target="tpu_custom_call" | custom-call | tf_op jit(solution)/shard_map/pallas_call | solution.py:339
  6.4 41.8 %all_to_all.10.in_ref = bf16[128,64,128]{2,1,0:T(8,128)(2,1)} all-to-all(bf16[128,64,128]{2,1,0:T(8,128)(2,1)} %shard_map.67), channel_id=1, replica_groups=mesh['step'=8,'space'=16] {'step','space'}, dimensions={0} | all-to-all | bytes 4194304 | tf_op jit(solution)/shard_map/all_to_all | solution.py:346
  48.2 21.6 %shard_map.68 = f32[3584,128]{1,0:T(8,128)} custom-call(bf16[128,64,128]{2,1,0:T(8,128)(2,1)} %all_to_all.10.in_ref), custom_call_target="tpu_custom_call" | custom-call | tf_op jit(solution)/shard_map/pallas_call | solution.py:348
  69.8 1.6 %convert_element_type.7 = f16[3584,128]{1,0:T(8,128)(2,1)S(1)} convert(f32[3584,128]{1,0:T(8,128)} %shard_map.68) | non-fusion elementwise | flops 458752 | bytes 2752512 | tf_op jit(solution)/shard_map/convert_element_type | solution.py:363
  71.4 22.0 %all_to_all.11 = f16[128,7,4,128]{3,2,1,0:T(4,128)(2,1)S(1)} all-to-all(f16[128,7,4,128]{3,2,1,0:T(4,128)(2,1)S(1)} %bitcast.3), channel_id=1, replica_groups=mesh['step'=8,'space'=16] {'step','space'}, dimensions={0} | all-to-all | bytes 1835008 | tf_op jit(solution)/shard_map/all_to_all | solution.py:364
  93.4 1.4 %convert.1.in_ref = f32[3584,128]{1,0:T(8,128)} convert(f16[3584,128]{1,0:T(8,128)(2,1)S(1)} %bitcast.4) | non-fusion elementwise | flops 458752 | bytes 2752512 | tf_op jit(solution)/shard_map/reshape | solution.py:365
  94.8 5.7 %shard_map.69 = (f32[2,1,256,256]{3,2,1,0:T(8,128)}, f32[2,1,256,256]{3,2,1,0:T(8,128)}, f32[1,3,1,256,256]{4,3,2,1,0:T(8,128)}) custom-call(f32[3584,128]{1,0:T(8,128)} %convert.1.in_ref), custom_call_target="tpu_custom_call" | custom-call | tf_op jit(solution)/shard_map/pallas_call | solution.py:366

commit v3 on v2

--- a/solution.py
+++ b/solution.py
@@ -10,6 +10,7 @@
 SIDE = 256
 PAIRS = 16
 STEPS = 8
+TOGETHER = 2
 OWN_Y = 32
 OWN_X = 16
 HALO = 2 * WIN
@@ -171,11 +172,11 @@
 
     scale = spread_of(1.0)
 
-    def put(vectors, row, factor):
-        for zo in range(2):
-            for gg in range(4):
-                value = jnp.where(mine, vectors[zo, 2 * gg], pltpu.roll(vectors[zo, 2 * gg + 1], OWN_X, 1))
-                out_ref[pl.ds(row + OUT_ROWS * zo + gg, 8, stride=2 * OUT_ROWS), :] = value * factor
+    def put_pair(vectors, zo, g, row, factor):
+        even, odd = (zo, g - g % 2), (zo, g - g % 2 + 1)
+        if g < OWN and even in vectors and odd in vectors:
+            value = jnp.where(mine, vectors[even], pltpu.roll(vectors[odd], OWN_X, 1))
+            out_ref[pl.ds(row + OUT_ROWS * zo + g // 2, 8, stride=2 * OUT_ROWS), :] = value * factor
 
     def from_below(g, zo, v):
         if g == 7:
@@ -198,98 +199,110 @@
     needs[11] = {11, 10, 0, 8}
     order = (7, 11, 8, 0, 1, 2, 3, 4, 5, 6, 9, 10)
 
-    def one_pair(p, carry):
-        owner = p // 2
-        base = owner * 12
-        which = p % 2
-        start = table_ref[base + 2 * which]
-        target = table_ref[base + 2 * which + 1]
-        steps = [table_ref[base + 4 + 4 * which + k] for k in range(WIN)]
-        out_row = owner * (NZ * OUT_ROWS) + 4 * which
-
-        def state(k, i):
-            return snap_ref[start, i] if k == 0 else rho_ref[k - 1, i]
-
+    def forward(c, k):
+        step = c["steps"][k]
+        mids, ups, downs, finals = {}, {}, {}, {}
+        done, todo = set(), list(order)
+        for g in order:
+            zp, zm = [], []
+            for zo in range(2):
+                i = zo * GROUPS + g
+                rho = c["state"](k, i)
+                both = (2.0 * near) * rho
+                xp = drift_ref[step, 0, i] * rho
+                yp = drift_ref[step, 1, i] * rho
+                zp.append(drift_ref[step, 2, i] * rho)
+                zm.append(both - zp[zo])
+                downs[zo, g] = both - yp
+                ups[zo, g] = yp
+                mids[zo, g] = keep * rho + (pltpu.roll(both - xp, 127, 1) + pltpu.roll(xp, 1, 1))
+            mids[0, g] += zm[1] + jnp.where(first, zero, pltpu.roll(zp[1], 1, 0))
+            mids[1, g] += zp[0] + jnp.where(last, zero, pltpu.roll(zm[0], 7, 0))
+            done.add(g)
+            for d in [d for d in todo if needs[d] & set(order) <= done]:
+                todo.remove(d)
+                for zo in range(2):
+                    value = mids[zo, d] + (from_below(d, zo, downs) + from_above(d, zo, ups))
+                    i = zo * GROUPS + d
+                    if k < WIN - 1:
+                        c["rho"][k, i] = value
+                    else:
+                        c["lam"][0, i] = value - snap_ref[c["target"], i]
+                        finals[zo, d] = value
+                    if k == WIN - 1:
+                        put_pair(finals, zo, d, c["row"], scale)
+
+    def backward(c, index):
+        k = WIN - 1 - index
+        step = c["steps"][k]
+        source, sink = index % 2, 1 - index % 2
+        wanted = [g for g in order if g < OWN or index < 2 or (index == 2 and g in (8, 11))]
+        fields, finals = {}, {}
+        done, todo = set(), list(wanted)
+        for g in [g for g in order if index < 3 or g not in (9, 10)]:
+            for zo in range(2):
+                fields[zo, g] = c["lam"][source, zo * GROUPS + g]
+            done.add(g)
+            for d in [d for d in todo if needs[d] & set(order) <= done]:
+                todo.remove(d)
+                zn = fields[1, d], jnp.where(last, zero, pltpu.roll(fields[0, d], 7, 0))
+                zq = jnp.where(first, zero, pltpu.roll(fields[1, d], 1, 0)), fields[0, d]
+                for zo in range(2):
+                    i = zo * GROUPS + d
+                    lam = fields[zo, d]
+                    xn, xq = pltpu.roll(lam, 127, 1), pltpu.roll(lam, 1, 1)
+                    yn, yq = from_below(d, zo, fields), from_above(d, zo, fields)
+                    dx, dy, dz = xn - xq, yn - yq, zn[zo] - zq[zo]
+                    value = (
+                        (keep * lam + (2.0 * near) * (xq + yq + zq[zo]))
+                        + (drift_ref[step, 0, i] * dx + drift_ref[step, 1, i] * dy)
+                        + drift_ref[step, 2, i] * dz
+                    )
+                    if index < WIN - 1:
+                        c["lam"][sink, i] = value
+                    else:
+                        finals[zo, d] = value
+                        put_pair(finals, zo, d, c["row"] + 8, scale)
+                    if d < OWN:
+                        rho = c["state"](k, i)
+                        for n, slope in enumerate((dx, dy, dz)):
+                            grad_ref[step * 3 + n, zo * OWN + d] += rho * slope
+
+    def pairs_of(i, carry):
+        cases = []
+        for n in range(TOGETHER):
+            p = TOGETHER * i + n
+            owner = p // 2
+            base = owner * 12
+            which = p % 2
+            start = table_ref[base + 2 * which]
+            rho, lam = rho_ref.at[n], lam_ref.at[n]
+            cases.append(
+                {
+                    "target": table_ref[base + 2 * which + 1],
+                    "steps": [table_ref[base + 4 + 4 * which + k] for k in range(WIN)],
+                    "row": owner * (NZ * OUT_ROWS) + 4 * which,
+                    "rho": rho,
+                    "lam": lam,
+                    "state": lambda k, i, rho=rho, start=start: snap_ref[start, i] if k == 0 else rho[k - 1, i],
+                }
+            )
         for k in range(WIN):
-            step = steps[k]
-            mids, ups, downs, finals = {}, {}, {}, {}
-            done, todo = set(), list(order)
-            for g in order:
-                zp, zm = [], []
-                for zo in range(2):
-                    i = zo * GROUPS + g
-                    rho = state(k, i)
-                    both = (2.0 * near) * rho
-                    xp = drift_ref[step, 0, i] * rho
-                    yp = drift_ref[step, 1, i] * rho
-                    zp.append(drift_ref[step, 2, i] * rho)
-                    zm.append(both - zp[zo])
-                    downs[zo, g] = both - yp
-                    ups[zo, g] = yp
-                    mids[zo, g] = keep * rho + (pltpu.roll(both - xp, 127, 1) + pltpu.roll(xp, 1, 1))
-                mids[0, g] += zm[1] + jnp.where(first, zero, pltpu.roll(zp[1], 1, 0))
-                mids[1, g] += zp[0] + jnp.where(last, zero, pltpu.roll(zm[0], 7, 0))
-                done.add(g)
-                for d in [d for d in todo if needs[d] & set(order) <= done]:
-                    todo.remove(d)
-                    for zo in range(2):
-                        value = mids[zo, d] + (from_below(d, zo, downs) + from_above(d, zo, ups))
-                        i = zo * GROUPS + d
-                        if k < WIN - 1:
-                            rho_ref[k, i] = value
-                        else:
-                            lam_ref[0, i] = value - snap_ref[target, i]
-                            finals[zo, d] = value
-            if k == WIN - 1:
-                put(finals, out_row, scale)
-
+            for c in cases:
+                forward(c, k)
         for index in range(WIN):
-            k = WIN - 1 - index
-            step = steps[k]
-            source, sink = index % 2, 1 - index % 2
-            wanted = [g for g in order if g < OWN or index < 2 or (index == 2 and g in (8, 11))]
-            fields, finals = {}, {}
-            done, todo = set(), list(wanted)
-            for g in [g for g in order if index < 3 or g not in (9, 10)]:
-                for zo in range(2):
-                    fields[zo, g] = lam_ref[source, zo * GROUPS + g]
-                done.add(g)
-                for d in [d for d in todo if needs[d] & set(order) <= done]:
-                    todo.remove(d)
-                    zn = fields[1, d], jnp.where(last, zero, pltpu.roll(fields[0, d], 7, 0))
-                    zq = jnp.where(first, zero, pltpu.roll(fields[1, d], 1, 0)), fields[0, d]
-                    for zo in range(2):
-                        i = zo * GROUPS + d
-                        lam = fields[zo, d]
-                        xn, xq = pltpu.roll(lam, 127, 1), pltpu.roll(lam, 1, 1)
-                        yn, yq = from_below(d, zo, fields), from_above(d, zo, fields)
-                        dx, dy, dz = xn - xq, yn - yq, zn[zo] - zq[zo]
-                        value = (
-                            (keep * lam + (2.0 * near) * (xq + yq + zq[zo]))
-                            + (drift_ref[step, 0, i] * dx + drift_ref[step, 1, i] * dy)
-                            + drift_ref[step, 2, i] * dz
-                        )
-                        if index < WIN - 1:
-                            lam_ref[sink, i] = value
-                        else:
-                            finals[zo, d] = value
-                        if d < OWN:
-                            rho = state(k, i)
-                            for c, slope in enumerate((dx, dy, dz)):
-                                grad_ref[step * 3 + c, zo * OWN + d] += rho * slope
-            if index == WIN - 1:
-                put(finals, out_row + 8, scale)
-        return carry
-
-    lax.fori_loop(0, PAIRS, one_pair, 0)
-
-    def store_grads(s, carry):
+            for c in cases:
+                backward(c, index)
+        return carry
+
+    lax.fori_loop(0, PAIRS // TOGETHER, pairs_of, 0)
+
+    for s in range(STEPS):
         for c in range(3):
-            own = {(zo, g): grad_ref[s * 3 + c, zo * OWN + g] for zo in range(2) for g in range(OWN)}
-            put(own, s * (NZ * OUT_ROWS) + 16 + 4 * c, half * scale)
-        return carry
-
-    lax.fori_loop(0, STEPS, store_grads, 0)
+            for zo in range(2):
+                own = {(zo, g): grad_ref[s * 3 + c, zo * OWN + g] for g in range(OWN)}
+                for g in range(0, OWN, 2):
+                    put_pair(own, zo, g, s * (NZ * OUT_ROWS) + 16 + 4 * c, half * scale)
 
 
 def planes_kernel(in_ref, final_ref, adjoint_ref, grad_ref, plane_ref):
@@ -336,12 +349,14 @@
     f32, bf16, f16 = jnp.float32, jnp.bfloat16, jnp.float16
     smem = pl.BlockSpec(memory_space=pltpu.SMEM)
     vmem = pl.BlockSpec(memory_space=pltpu.VMEM)
+    limit = pltpu.CompilerParams(vmem_limit_bytes=16 << 20)
     windows = pl.pallas_call(
         build_kernel,
         out_shape=jax.ShapeDtypeStruct((128, IN_ROWS, 128), bf16),
         in_specs=[smem, smem, vmem, vmem],
         out_specs=vmem,
         scratch_shapes=[pltpu.VMEM((4, 16, 64, 128), f32)],
+        compiler_params=limit,
     )(pair_table, plan, snapshots, drift)
     windows = lax.all_to_all(windows, ("step", "space"), 0, 0, tiled=True)
     groups = 2 * GROUPS
@@ -354,11 +369,12 @@
             pltpu.VMEM((NZ * PLANE_ROWS, 128), f32),
             pltpu.VMEM((STEPS, groups) + VREG, f32),
             pltpu.VMEM((STEPS, 3, groups) + VREG, f32),
-            pltpu.VMEM((WIN - 1, groups) + VREG, f32),
-            pltpu.VMEM((2, groups) + VREG, f32),
+            pltpu.VMEM((TOGETHER, WIN - 1, groups) + VREG, f32),
+            pltpu.VMEM((TOGETHER, 2, groups) + VREG, f32),
             pltpu.VMEM((STEPS * 3, 2 * OWN) + VREG, f32),
             pltpu.SMEM((STEPS * 12,), jnp.int32),
         ],
+        compiler_params=limit,
     )(windows)
     results = results.reshape(128, OUT_ROWS // 4, 4, 128).astype(f16)
     results = lax.all_to_all(results, ("step", "space"), 0, 0, tiled=True)
@@ -373,6 +389,7 @@
         in_specs=[vmem],
         out_specs=(vmem, vmem, vmem),
         scratch_shapes=[pltpu.VMEM((7, 2, OWN_Y, 128), f32)],
+        compiler_params=limit,
     )(results)
 
 

time: 101 us -> 92 us (0.911)
  Pallas kernels: 33.2 us -> 24.1 us
  local copies, waits for them, and re-layouts: 0 us -> 3.3 us
  other arithmetic: 2.99 us -> 0.24 us
    pallas_call x1, Pallas kernels: 21.6 us -> 15.9 us  [local(): pl.pallas_call(window_kernel, out_shape=jax.ShapeDtypeStruct((128 * OUT_R...]
    unnamed x0 -> x8, local copies, waits for them, and re-layouts: none -> 3.3 us
    pallas_call x1, Pallas kernels: 5.76 us -> 3.93 us  [local(): pl.pallas_call(build_kernel, out_shape=jax.ShapeDtypeStruct((128, IN_ROWS...]
    pallas_call x1, Pallas kernels: 5.75 us -> 4.25 us  [local(): pl.pallas_call(planes_kernel, out_shape=(jax.ShapeDtypeStruct((2, 1, SIDE...]
    convert_element_type x1, other arithmetic: 1.62 us -> 0.12 us  [local(): results = results.reshape(128, OUT_ROWS // 4, 4, 128).astype(f16)]
    reshape x1, other arithmetic: 1.37 us -> 0.12 us  [local(): results = results.astype(f32).reshape(128 * OUT_ROWS, 128)]
where the time goes in v3:
time: 92 us; the launch traced here: 91.8 us
  blocking collectives  63.4 us (69%)
  Pallas kernels  24.1 us (26%)
  local copies, waits for them, and re-layouts  3.3 us (4%)
    all_to_all x1, blocking collectives, local(): windows = lax.all_to_all(windows, ('step', 'space'), 0, 0, tiled=True)  41.5 us
    all_to_all x1, blocking collectives, local(): results = lax.all_to_all(results, ('step', 'space'), 0, 0, tiled=True)  22 us
    pallas_call x1, Pallas kernels, local(): pl.pallas_call(window_kernel, out_shape=jax.ShapeDtypeStruct((128 * OUT_R...  15.9 us
    pallas_call x1, Pallas kernels, local(): pl.pallas_call(planes_kernel, out_shape=(jax.ShapeDtypeStruct((2, 1, SIDE...  4.25 us
    pallas_call x1, Pallas kernels, local(): pl.pallas_call(build_kernel, out_shape=jax.ShapeDtypeStruct((128, IN_ROWS...  3.93 us
    unnamed x8, local copies, waits for them, and re-layouts  3.3 us

profile of v3, /device:TPU:1, one launch (start us, length us, event | category | flops | bytes accessed | tf_op | source)
XLA Modules:
  0.0 91.8 jit_solution(15387528877582647873)
XLA Ops:
  0.6 0.0 copy-start
  0.6 1.0 %copy-done = bf16[1,3,1,256,256]{4,3,2,1,0:T(8,128)(2,1)S(1)} copy-done((bf16[1,3,1,256,256]{4,3,2,1,0:T(8,128)(2,1)S(1)}, bf16[1,3,1,256,256]{4,3,2,1,0:T(8,128)(2,1)}, u32[]{:S(2)}) %copy-start) | copy-done | bytes 393240
  1.6 0.0 copy-start.1
  1.6 0.9 %copy-done.1 = f32[1,1,256,256]{3,2,1,0:T(8,128)S(1)} copy-done((f32[1,1,256,256]{3,2,1,0:T(8,128)S(1)}, f32[1,1,256,256]{3,2,1,0:T(8,128)}, u32[]{:S(2)}) %copy-start.1) | copy-done | bytes 262168
  2.6 0.0 copy-start.2
  2.6 0.7 copy-done.2
  3.3 0.0 copy-start.3
  3.3 0.7 copy-done.3
  3.9 3.9 %shard_map.67 = bf16[128,64,128]{2,1,0:T(8,128)(2,1)S(1)} custom-call(s32[2,2]{1,0:T(2,128)S(1)} %copy-done.2, s32[2,4]{1,0:T(2,128)S(1)} %copy-done.3, f32[1,1,256,256]{3,2,1,0:T(8,128)S(1)} %copy-done.1, bf16[1,3,1,256,256]{4,3,2,1,0:T(8,128)(2,1)S(1)} %copy-done), custom_call_target="tpu_custom_call" | custom-call | tf_op jit(solution)/shard_map/pallas_call | solution.py:353
  7.9 41.5 %all_to_all.10.in_ref = bf16[128,64,128]{2,1,0:T(8,128)(2,1)S(1)} all-to-all(bf16[128,64,128]{2,1,0:T(8,128)(2,1)S(1)} %shard_map.67), channel_id=1, replica_groups=mesh['step'=8,'space'=16] {'step','space'}, dimensions={0} | all-to-all | bytes 4194304 | tf_op jit(solution)/shard_map/all_to_all | solution.py:361
  49.4 15.9 %shard_map.68 = f32[3584,128]{1,0:T(8,128)S(1)} custom-call(bf16[128,64,128]{2,1,0:T(8,128)(2,1)S(1)} %all_to_all.10.in_ref), custom_call_target="tpu_custom_call" | custom-call | tf_op jit(solution)/shard_map/pallas_call | solution.py:363
  65.3 0.1 convert_element_type.7
  65.4 22.0 %all_to_all.11 = f16[128,7,4,128]{3,2,1,0:T(4,128)(2,1)S(1)} all-to-all(f16[128,7,4,128]{3,2,1,0:T(4,128)(2,1)S(1)} %bitcast.3), channel_id=1, replica_groups=mesh['step'=8,'space'=16] {'step','space'}, dimensions={0} | all-to-all | bytes 1835008 | tf_op jit(solution)/shard_map/all_to_all | solution.py:380
  87.4 0.1 convert.1.in_ref
  87.5 4.3 %shard_map.69 = (f32[2,1,256,256]{3,2,1,0:T(8,128)}, f32[2,1,256,256]{3,2,1,0:T(8,128)}, f32[1,3,1,256,256]{4,3,2,1,0:T(8,128)}) custom-call(f32[3584,128]{1,0:T(8,128)S(1)} %convert.1.in_ref), custom_call_target="tpu_custom_call" | custom-call | tf_op jit(solution)/shard_map/pallas_call | solution.py:382
Async XLA Ops:
  0.6 1.0 %copy-start = (bf16[1,3,1,256,256]{4,3,2,1,0:T(8,128)(2,1)S(1)}, bf16[1,3,1,256,256]{4,3,2,1,0:T(8,128)(2,1)}, u32[]{:S(2)}) copy-start(bf16[1,3,1,256,256]{4,3,2,1,0:T(8,128)(2,1)} %drift_ref.1) | copy-start | bytes 1179652
  1.6 0.9 %copy-start.1 = (f32[1,1,256,256]{3,2,1,0:T(8,128)S(1)}, f32[1,1,256,256]{3,2,1,0:T(8,128)}, u32[]{:S(2)}) copy-start(f32[1,1,256,256]{3,2,1,0:T(8,128)} %snap_ref.1) | copy-start | bytes 786436
  2.6 0.7 copy-start.2
  3.3 0.7 copy-start.3
